TPU v7x, 256 devices: a whole 4x4x8 slice. The times are simulated.
256 devices in a mesh: req: 16 (over y_lo, z), tensor: 16 (over y_hi, x, core).
Axes of the slice: x: 4, y: 4 (y_hi: 2, y_lo: 2; y = y_hi * 2 + y_lo), z: 8, core: 2. Of those that a mesh axis runs over, the one named last changes fastest.
Arguments:
- activations: bfloat16 [8192, 8192], P(('req', 'tensor')), parts along dimension 0, may hold values from -6 to 6
- norm_gain: float32 [8192], replicated, may hold values from 0.1 to 1.9
- query_weight: bfloat16 [8192, 4096], P(None, 'tensor'), may hold values from -0.0625 to 0.0625
- keyvalue_weight: bfloat16 [8192, 2048], P(None, 'tensor'), may hold values from -0.0625 to 0.0625
- output_weight: bfloat16 [4096, 8192], P('tensor'), may hold values from -0.09375 to 0.09375
- page_pool: bfloat16 [2048, 128, 256], P(('req', 'tensor')), parts along dimension 0, may hold values from -320 to 320
- page_table: int32 [288, 8], P('req'), parts along dimension 0, may hold values from 0 to 15
- prefill_offsets: int32 [32], P('req'), parts along dimension 0, may hold values from 0 to 1024, as said below
- decode_lengths: int32 [256], P('req'), parts along dimension 0, may hold values from 1 to 1024, as said below
Outputs:
- block_output: bfloat16 [8192, 8192], P(('req', 'tensor')), parts along dimension 0
There are 16 independent parts, one for each index of `req`. A program takes and returns all parts, laid end to end along the dimension named above; an argument that names none is the same for every part. Nothing has to cross between parts.
Inputs may be any that keep to these rules, and one draw needn't show every extreme that they name: `page_table`: pages may be shared between requests. `decode_lengths`: some decode request has exactly 1024 cached tokens. `prefill_offsets`: some stretch has exactly 1024 cached tokens before it.
All inputs are finite; a program needn't handle non-finite values.
Results may differ from a plain program's by a relative error of at most 0.0095.
The roundings to bfloat16 on the way count: a program that leaves them out, or rounds other values in their place, can miss the bound.
Values may be sent and summed in bfloat16 or wider, within the bound.
A program may use at most 128 MiB of HBM per device.

v0:
```python
import jax
import jax.numpy as jnp
from jax import lax
from jax.sharding import PartitionSpec as P

QH = 32
KVH = 8
HD = 128
C = 248
eps_norm = 1e-06
rope_base = 1000000.0
neg_big = -1e30


def partner(array, axis, distance):
    return lax.ppermute(array, axis, [(i, i ^ 1 << distance) for i in range(lax.axis_size(axis))])


def rotate(values, positions):
    half_dim = values.shape[-1] // 2
    frequency = rope_base ** (-2.0 * jnp.arange(half_dim, dtype=jnp.float32) / values.shape[-1])
    angles = positions.astype(jnp.float32)[:, None] * frequency[None, :]
    cosine = jnp.cos(angles)[:, None, :]
    sine_part = jnp.sin(angles)[:, None, :]
    first_half = values[..., :half_dim]
    second_half = values[..., half_dim:]
    return jnp.concatenate(
        [
            first_half * cosine - second_half * sine_part,
            second_half * cosine + first_half * sine_part,
        ],
        axis=-1,
    )


def cached_block(queries, table_row, key_limit, pool_rows, page_lo):
    held_pages = pool_rows.shape[1]
    page_len = pool_rows.shape[2]
    head_dim = queries.shape[-1]
    local_page = table_row - page_lo
    owned_page = (local_page >= 0) & (local_page < held_pages)
    local_page = jnp.clip(local_page, 0, held_pages - 1)
    fetched = jnp.take(pool_rows, local_page, axis=1)
    key_span = fetched.shape[1] * page_len
    key_rows = fetched.reshape(pool_rows.shape[0], key_span, 2 * head_dim)
    slot_ids = jnp.arange(key_span, dtype=jnp.int32)
    visible = jnp.repeat(owned_page, page_len, total_repeat_length=key_span) & (
        slot_ids < key_limit
    )
    scores = jnp.einsum(
        "rkgd,ksd->kgrs", queries, key_rows[:, :, :head_dim], preferred_element_type=jnp.float32
    ) * head_dim ** (-0.5)
    scores = jnp.where(visible, scores, neg_big)
    highest = jnp.max(scores, axis=-1)
    weights = jnp.where(visible, jnp.exp(scores - highest[..., None]), 0.0)
    totals = jnp.sum(weights, axis=-1)
    blended = jnp.einsum(
        "kgrs,ksd->rkgd",
        weights.astype(jnp.bfloat16),
        key_rows[:, :, head_dim:],
        preferred_element_type=jnp.float32,
    )
    return (jnp.transpose(highest, (2, 0, 1)), jnp.transpose(totals, (2, 0, 1)), blended)


def cached_all(
    queries, pool_rows, page_lo, page_table, prefill_offsets, decode_lengths, stretch_len
):
    pieces = []
    for stretch_id in range(2):
        lower = stretch_id * stretch_len
        pieces.append(
            cached_block(
                queries[lower : lower + stretch_len],
                page_table[stretch_id],
                prefill_offsets[stretch_id],
                pool_rows,
                page_lo,
            )
        )

    def decode_one(decode_item):
        query_row, table_row, length_one = decode_item
        return cached_block(query_row[None], table_row, length_one, pool_rows, page_lo)

    decoded = lax.map(decode_one, (queries[2 * stretch_len :], page_table[2:], decode_lengths))
    decoded = tuple((stacked[:, 0] for stacked in decoded))
    return tuple(
        (
            jnp.concatenate([pieces[0][part_id], pieces[1][part_id], decoded[part_id]], axis=0)
            for part_id in range(3)
        )
    )


def stretch_self(queries, new_keys, new_values):
    length_q = queries.shape[0]
    scores = jnp.einsum(
        "rkgd,skd->kgrs", queries, new_keys, preferred_element_type=jnp.float32
    ) * queries.shape[-1] ** (-0.5)
    counter = jnp.arange(length_q, dtype=jnp.int32)
    causal = counter[:, None] >= counter[None, :]
    scores = jnp.where(causal, scores, neg_big)
    highest = jnp.max(scores, axis=-1)
    weights = jnp.where(causal, jnp.exp(scores - highest[..., None]), 0.0)
    totals = jnp.sum(weights, axis=-1)
    blended = jnp.einsum(
        "kgrs,skd->rkgd",
        weights.astype(jnp.bfloat16),
        new_values,
        preferred_element_type=jnp.float32,
    )
    return (jnp.transpose(highest, (2, 0, 1)), jnp.transpose(totals, (2, 0, 1)), blended)


def fresh_all(queries, new_keys, new_values, stretch_len):
    pieces = []
    for stretch_id in range(2):
        lower = stretch_id * stretch_len
        upper = lower + stretch_len
        pieces.append(
            stretch_self(queries[lower:upper], new_keys[lower:upper], new_values[lower:upper])
        )
    tail_q = queries[2 * stretch_len :]
    own_score = jnp.einsum(
        "rkgd,rkd->rkg", tail_q, new_keys[2 * stretch_len :], preferred_element_type=jnp.float32
    ) * queries.shape[-1] ** (-0.5)
    own_values = jnp.broadcast_to(
        new_values[2 * stretch_len :].astype(jnp.float32)[:, :, None, :], tail_q.shape
    )
    decoded = (own_score, jnp.ones_like(own_score), own_values)
    return tuple(
        (
            jnp.concatenate([pieces[0][part_id], pieces[1][part_id], decoded[part_id]], axis=0)
            for part_id in range(3)
        )
    )


def combine_parts(first, second):
    highest = jnp.maximum(first[0], second[0])
    first_scale = jnp.exp(first[0] - highest)
    second_scale = jnp.exp(second[0] - highest)
    totals = first_scale * first[1] + second_scale * second[1]
    blended = first_scale[..., None] * first[2] + second_scale[..., None] * second[2]
    return (highest, totals, blended)


def shards(
    activations,
    norm_gain,
    query_weight,
    keyvalue_weight,
    output_weight,
    page_pool,
    page_table,
    prefill_offsets,
    decode_lengths,
):
    my_index = lax.axis_index("tensor")
    parity = my_index % 2
    local_q = query_weight.shape[1] // HD
    group = QH // KVH
    widened = activations.astype(jnp.float32)
    normed = (
        widened
        * lax.rsqrt(jnp.mean(widened * widened, axis=-1, keepdims=True) + eps_norm)
        * norm_gain
    ).astype(jnp.bfloat16)
    project_piece = lax.all_gather(normed, "tensor", axis=0, tiled=True)
    joint = jnp.concatenate(
        [
            jnp.dot(project_piece, query_weight, preferred_element_type=jnp.float32),
            jnp.dot(project_piece, keyvalue_weight, preferred_element_type=jnp.float32),
        ],
        axis=1,
    )
    row_count = joint.shape[0]
    inner = jnp.arange(C, dtype=jnp.int32)
    positions = jnp.concatenate(
        [prefill_offsets[0] + inner, prefill_offsets[1] + inner, decode_lengths]
    )
    own_q = rotate(joint[:, : local_q * HD].reshape(row_count, local_q, HD), positions).astype(
        jnp.bfloat16
    )
    kv_cols = joint[:, local_q * HD :]
    kv_local = 1
    turned = rotate(kv_cols[:, None, :], positions)[:, 0, :]
    own_half = jnp.where(parity == 0, turned, kv_cols).astype(jnp.bfloat16)
    other_half = partner(own_half, "tensor", 0)
    new_keys = jnp.where(parity == 0, own_half, other_half)[:, None, :]
    new_values = jnp.where(parity == 0, other_half, own_half)[:, None, :]
    local_pool = page_pool[None]
    own_grouped = own_q.reshape(row_count, kv_local, local_q // kv_local, HD)
    other_q = partner(own_q, "tensor", 0)
    lower_first = jnp.concatenate([own_q, other_q], axis=1)
    upper_first = jnp.concatenate([other_q, own_q], axis=1)
    group_q = jnp.where(parity == 0, lower_first, upper_first).reshape(row_count, 1, group, HD)
    found = cached_all(
        group_q,
        local_pool,
        parity * page_pool.shape[0],
        page_table,
        prefill_offsets,
        decode_lengths,
        C,
    )
    low_part = tuple((piece[:, :, :local_q] for piece in found))
    high_part = tuple((piece[:, :, local_q:] for piece in found))
    mine = tuple(
        (
            jnp.where(parity == 0, low_piece, high_piece)
            for low_piece, high_piece in zip(low_part, high_part)
        )
    )
    theirs = tuple(
        (
            jnp.where(parity == 0, high_piece, low_piece)
            for low_piece, high_piece in zip(low_part, high_part)
        )
    )
    received = partner((theirs[0], theirs[1], theirs[2]), "tensor", 0)
    cached = combine_parts(mine, received)
    fresh = fresh_all(own_grouped, new_keys, new_values, C)
    highest, totals, blended = combine_parts(cached, fresh)
    attended = (blended / totals[..., None]).astype(jnp.bfloat16).reshape(row_count, local_q * HD)
    piece = attended
    summed = lax.psum_scatter(
        jnp.dot(piece, output_weight, preferred_element_type=jnp.float32),
        "tensor",
        scatter_dimension=0,
        tiled=True,
    )
    return summed.astype(jnp.bfloat16)


def solution(mesh):
    placed = (
        P(("req", "tensor"), None),
        P(),
        P(None, "tensor"),
        P(None, "tensor"),
        P("tensor", None),
        P(("req", "tensor"), None, None),
        P("req", None),
        P("req"),
        P("req"),
    )
    return jax.shard_map(
        shards, mesh=mesh, in_specs=placed, out_specs=P(("req", "tensor"), None), check_vma=False
    )
```

profile of v0, /device:TPU:1, one launch (start us, length us, event | category | flops | bytes accessed | tf_op | source)
XLA Modules:
  0.0 439.1 jit_solution(1664595664184705682)
XLA Ops:
  6.6 1.4 fusion.62
  8.0 2.0 fusion.64
  11.0 1.0 clamp_reduce_fusion.1
  12.0 1.6 gather_fusion.1
  13.6 1.6 gather_fusion.2
  17.4 5.5 %fusion.116 = pred[1024]{0:T(1024)(128)(4,1)S(1)} fusion(s32[]{:T(128)} %bitcast.35, pred[]{:T(512)} %bitcast.34, pred[]{:T(512)} %bitcast.33, pred[]{:T(512)} %bitcast.32, pred[]{:T(512)} %bitcast.31, pred[]{:T(512)} %bitcast.30, pred[]{:T(512)} %bitcast.29, pred[]{:T(512)} %bitcast.28, pred[]{:T(512)} %bitcast.27), kind=kLoop, calls=%fused_computation.187 | loop fusion | flops 25600 | bytes 1036 | tf_op jit(solution)/shard_map/and | solution.py:47
  23.0 5.6 %fusion.117 = pred[1024]{0:T(1024)(128)(4,1)S(1)} fusion(s32[]{:T(128)} %bitcast.42, pred[]{:T(512)} %bitcast.54, pred[]{:T(512)} %bitcast.53, pred[]{:T(512)} %bitcast.52, pred[]{:T(512)} %bitcast.51, pred[]{:T(512)} %bitcast.50, pred[]{:T(512)} %bitcast.49, pred[]{:T(512)} %bitcast.48, pred[]{:T(512)} %bitcast.47), kind=kLoop, calls=%fused_computation.188 | loop fusion | flops 25600 | bytes 1036 | tf_op jit(solution)/shard_map/and | solution.py:47
  28.5 1.2 iota_add_fusion
  29.9 1.8 multiply_cosine_fusion.1
  31.6 1.0 bitcast_select_fusion.4
  32.6 1.0 bitcast_select_fusion.3
  33.6 58.7 %all-gather.2.cloned.1.call-done = bf16[512,8192]{1,0:T(8,128)(2,1)} async-done(((bf16[32,8192]{1,0:T(8,128)(2,1)}), bf16[512,8192]{1,0:T(8,128)(2,1)}) %all-gather.2.cloned.1.call-update) | async-done | bytes 8388624 | tf_op jit(solution)/shard_map/all_gather | solution.py:170
  92.3 6.9 %fusion.141 = f32[512,256]{0,1:T(8,128)S(1)} fusion(bf16[512,8192]{1,0:T(8,128)(2,1)} %all-gather.2.cloned.1.call-done, bf16[8192,256]{1,0:T(8,128)(2,1)} %param.23), kind=kOutput, calls=%fused_computation.227 | convolution fusion | flops 2147483648 | bytes 13107200 | tf_op jit(solution)/shard_map/dot_general | solution.py:173
  99.5 5.7 %fusion.142 = f32[512,128]{1,0:T(8,128)S(1)} fusion(bf16[512,8192]{1,0:T(8,128)(2,1)} %all-gather.2.cloned.1.call-done, bf16[8192,128]{1,0:T(8,128)(2,1)S(1)} %copy-done), kind=kOutput, calls=%fused_computation.228 | convolution fusion | flops 1073741824 | bytes 10747904 | tf_op jit(solution)/shard_map/dot_general | solution.py:174
  105.2 1.2 fusion.76
  107.4 1.0 copy.37
  108.4 1.2 add_convert_fusion
  110.9 1.6 broadcast_select_fusion.1
  112.9 1.1 fusion.139
  114.2 1.4 convolution_bitcast_fusion
  115.7 1.3 fusion.68
  116.9 1.8 convolution_bitcast_fusion.1
  119.4 1.3 maximum_select_fusion
  121.6 1.8 fusion.54
  123.4 1.2 fusion.40
  125.4 1.8 fusion.57
  127.3 1.2 fusion.38
  128.5 134.0 %while.21 = (s32[]{:T(128)}, f32[16,1,1,4]{3,2,1,0:T(1,128)S(1)}, f32[16,1,1,4]{3,2,1,0:T(1,128)S(1)}, f32[16,1,1,4,128]{4,0,3,2,1:T(8,128)S(1)}, s32[16,8]{1,0:...) while((s32[]{:T(128)}, f32[16,1,1,4]{3,2,1,0:T(1,128)S(1)}, ...), condition=%wide.region_6.9_spmd, body=%wide.region_3.8_spmd.sunk | while | flops 2422874 | bytes 2688929 | solution.py:86
  129.8 5.5 %fusion.158 = pred[1024]{0:T(1024)(128)(4,1)S(1)} fusion(s32[]{:T(128)} %bitcast.422, pred[]{:T(512)} %bitcast.423, pred[]{:T(512)} %bitcast.424, pred[]{:T(512)} %bitcast.425, pred[]{:T(512)} %bitcast.426, pred[]{:T(512)} %bitcast.427, pred[]{:T(512)} %bitcast.428, pred[]{:T(512)} %bitcast.429, pred[]{:T(512)} %bitcast.430), kind=kLoop, calls=%fused_computation.37.clone.1 | loop fusion | flops 25600 | bytes 1036 | tf_op jit(solution)/shard_map/while/body/eval_jaxpr/and | solution.py:47
  138.2 5.5 %fusion.158 = pred[1024]{0:T(1024)(128)(4,1)S(1)} fusion(s32[]{:T(128)} %bitcast.422, pred[]{:T(512)} %bitcast.423, pred[]{:T(512)} %bitcast.424, pred[]{:T(512)} %bitcast.425, pred[]{:T(512)} %bitcast.426, pred[]{:T(512)} %bitcast.427, pred[]{:T(512)} %bitcast.428, pred[]{:T(512)} %bitcast.429, pred[]{:T(512)} %bitcast.430), kind=kLoop, calls=%fused_computation.37.clone.1 | loop fusion | flops 25600 | bytes 1036 | tf_op jit(solution)/shard_map/while/body/eval_jaxpr/and | solution.py:47
  146.6 5.5 %fusion.158 = pred[1024]{0:T(1024)(128)(4,1)S(1)} fusion(s32[]{:T(128)} %bitcast.422, pred[]{:T(512)} %bitcast.423, pred[]{:T(512)} %bitcast.424, pred[]{:T(512)} %bitcast.425, pred[]{:T(512)} %bitcast.426, pred[]{:T(512)} %bitcast.427, pred[]{:T(512)} %bitcast.428, pred[]{:T(512)} %bitcast.429, pred[]{:T(512)} %bitcast.430), kind=kLoop, calls=%fused_computation.37.clone.1 | loop fusion | flops 25600 | bytes 1036 | tf_op jit(solution)/shard_map/while/body/eval_jaxpr/and | solution.py:47
  154.9 5.5 %fusion.158 = pred[1024]{0:T(1024)(128)(4,1)S(1)} fusion(s32[]{:T(128)} %bitcast.422, pred[]{:T(512)} %bitcast.423, pred[]{:T(512)} %bitcast.424, pred[]{:T(512)} %bitcast.425, pred[]{:T(512)} %bitcast.426, pred[]{:T(512)} %bitcast.427, pred[]{:T(512)} %bitcast.428, pred[]{:T(512)} %bitcast.429, pred[]{:T(512)} %bitcast.430), kind=kLoop, calls=%fused_computation.37.clone.1 | loop fusion | flops 25600 | bytes 1036 | tf_op jit(solution)/shard_map/while/body/eval_jaxpr/and | solution.py:47
  163.3 5.5 %fusion.158 = pred[1024]{0:T(1024)(128)(4,1)S(1)} fusion(s32[]{:T(128)} %bitcast.422, pred[]{:T(512)} %bitcast.423, pred[]{:T(512)} %bitcast.424, pred[]{:T(512)} %bitcast.425, pred[]{:T(512)} %bitcast.426, pred[]{:T(512)} %bitcast.427, pred[]{:T(512)} %bitcast.428, pred[]{:T(512)} %bitcast.429, pred[]{:T(512)} %bitcast.430), kind=kLoop, calls=%fused_computation.37.clone.1 | loop fusion | flops 25600 | bytes 1036 | tf_op jit(solution)/shard_map/while/body/eval_jaxpr/and | solution.py:47
  171.7 5.5 %fusion.158 = pred[1024]{0:T(1024)(128)(4,1)S(1)} fusion(s32[]{:T(128)} %bitcast.422, pred[]{:T(512)} %bitcast.423, pred[]{:T(512)} %bitcast.424, pred[]{:T(512)} %bitcast.425, pred[]{:T(512)} %bitcast.426, pred[]{:T(512)} %bitcast.427, pred[]{:T(512)} %bitcast.428, pred[]{:T(512)} %bitcast.429, pred[]{:T(512)} %bitcast.430), kind=kLoop, calls=%fused_computation.37.clone.1 | loop fusion | flops 25600 | bytes 1036 | tf_op jit(solution)/shard_map/while/body/eval_jaxpr/and | solution.py:47
  180.1 5.5 %fusion.158 = pred[1024]{0:T(1024)(128)(4,1)S(1)} fusion(s32[]{:T(128)} %bitcast.422, pred[]{:T(512)} %bitcast.423, pred[]{:T(512)} %bitcast.424, pred[]{:T(512)} %bitcast.425, pred[]{:T(512)} %bitcast.426, pred[]{:T(512)} %bitcast.427, pred[]{:T(512)} %bitcast.428, pred[]{:T(512)} %bitcast.429, pred[]{:T(512)} %bitcast.430), kind=kLoop, calls=%fused_computation.37.clone.1 | loop fusion | flops 25600 | bytes 1036 | tf_op jit(solution)/shard_map/while/body/eval_jaxpr/and | solution.py:47
  188.4 5.5 %fusion.158 = pred[1024]{0:T(1024)(128)(4,1)S(1)} fusion(s32[]{:T(128)} %bitcast.422, pred[]{:T(512)} %bitcast.423, pred[]{:T(512)} %bitcast.424, pred[]{:T(512)} %bitcast.425, pred[]{:T(512)} %bitcast.426, pred[]{:T(512)} %bitcast.427, pred[]{:T(512)} %bitcast.428, pred[]{:T(512)} %bitcast.429, pred[]{:T(512)} %bitcast.430), kind=kLoop, calls=%fused_computation.37.clone.1 | loop fusion | flops 25600 | bytes 1036 | tf_op jit(solution)/shard_map/while/body/eval_jaxpr/and | solution.py:47
  196.8 5.5 %fusion.158 = pred[1024]{0:T(1024)(128)(4,1)S(1)} fusion(s32[]{:T(128)} %bitcast.422, pred[]{:T(512)} %bitcast.423, pred[]{:T(512)} %bitcast.424, pred[]{:T(512)} %bitcast.425, pred[]{:T(512)} %bitcast.426, pred[]{:T(512)} %bitcast.427, pred[]{:T(512)} %bitcast.428, pred[]{:T(512)} %bitcast.429, pred[]{:T(512)} %bitcast.430), kind=kLoop, calls=%fused_computation.37.clone.1 | loop fusion | flops 25600 | bytes 1036 | tf_op jit(solution)/shard_map/while/body/eval_jaxpr/and | solution.py:47
  205.2 5.5 %fusion.158 = pred[1024]{0:T(1024)(128)(4,1)S(1)} fusion(s32[]{:T(128)} %bitcast.422, pred[]{:T(512)} %bitcast.423, pred[]{:T(512)} %bitcast.424, pred[]{:T(512)} %bitcast.425, pred[]{:T(512)} %bitcast.426, pred[]{:T(512)} %bitcast.427, pred[]{:T(512)} %bitcast.428, pred[]{:T(512)} %bitcast.429, pred[]{:T(512)} %bitcast.430), kind=kLoop, calls=%fused_computation.37.clone.1 | loop fusion | flops 25600 | bytes 1036 | tf_op jit(solution)/shard_map/while/body/eval_jaxpr/and | solution.py:47
  213.6 5.5 %fusion.158 = pred[1024]{0:T(1024)(128)(4,1)S(1)} fusion(s32[]{:T(128)} %bitcast.422, pred[]{:T(512)} %bitcast.423, pred[]{:T(512)} %bitcast.424, pred[]{:T(512)} %bitcast.425, pred[]{:T(512)} %bitcast.426, pred[]{:T(512)} %bitcast.427, pred[]{:T(512)} %bitcast.428, pred[]{:T(512)} %bitcast.429, pred[]{:T(512)} %bitcast.430), kind=kLoop, calls=%fused_computation.37.clone.1 | loop fusion | flops 25600 | bytes 1036 | tf_op jit(solution)/shard_map/while/body/eval_jaxpr/and | solution.py:47
  221.9 5.5 %fusion.158 = pred[1024]{0:T(1024)(128)(4,1)S(1)} fusion(s32[]{:T(128)} %bitcast.422, pred[]{:T(512)} %bitcast.423, pred[]{:T(512)} %bitcast.424, pred[]{:T(512)} %bitcast.425, pred[]{:T(512)} %bitcast.426, pred[]{:T(512)} %bitcast.427, pred[]{:T(512)} %bitcast.428, pred[]{:T(512)} %bitcast.429, pred[]{:T(512)} %bitcast.430), kind=kLoop, calls=%fused_computation.37.clone.1 | loop fusion | flops 25600 | bytes 1036 | tf_op jit(solution)/shard_map/while/body/eval_jaxpr/and | solution.py:47
  230.3 5.5 %fusion.158 = pred[1024]{0:T(1024)(128)(4,1)S(1)} fusion(s32[]{:T(128)} %bitcast.422, pred[]{:T(512)} %bitcast.423, pred[]{:T(512)} %bitcast.424, pred[]{:T(512)} %bitcast.425, pred[]{:T(512)} %bitcast.426, pred[]{:T(512)} %bitcast.427, pred[]{:T(512)} %bitcast.428, pred[]{:T(512)} %bitcast.429, pred[]{:T(512)} %bitcast.430), kind=kLoop, calls=%fused_computation.37.clone.1 | loop fusion | flops 25600 | bytes 1036 | tf_op jit(solution)/shard_map/while/body/eval_jaxpr/and | solution.py:47
  238.7 5.5 %fusion.158 = pred[1024]{0:T(1024)(128)(4,1)S(1)} fusion(s32[]{:T(128)} %bitcast.422, pred[]{:T(512)} %bitcast.423, pred[]{:T(512)} %bitcast.424, pred[]{:T(512)} %bitcast.425, pred[]{:T(512)} %bitcast.426, pred[]{:T(512)} %bitcast.427, pred[]{:T(512)} %bitcast.428, pred[]{:T(512)} %bitcast.429, pred[]{:T(512)} %bitcast.430), kind=kLoop, calls=%fused_computation.37.clone.1 | loop fusion | flops 25600 | bytes 1036 | tf_op jit(solution)/shard_map/while/body/eval_jaxpr/and | solution.py:47
  247.1 5.5 %fusion.158 = pred[1024]{0:T(1024)(128)(4,1)S(1)} fusion(s32[]{:T(128)} %bitcast.422, pred[]{:T(512)} %bitcast.423, pred[]{:T(512)} %bitcast.424, pred[]{:T(512)} %bitcast.425, pred[]{:T(512)} %bitcast.426, pred[]{:T(512)} %bitcast.427, pred[]{:T(512)} %bitcast.428, pred[]{:T(512)} %bitcast.429, pred[]{:T(512)} %bitcast.430), kind=kLoop, calls=%fused_computation.37.clone.1 | loop fusion | flops 25600 | bytes 1036 | tf_op jit(solution)/shard_map/while/body/eval_jaxpr/and | solution.py:47
  255.4 5.5 %fusion.158 = pred[1024]{0:T(1024)(128)(4,1)S(1)} fusion(s32[]{:T(128)} %bitcast.422, pred[]{:T(512)} %bitcast.423, pred[]{:T(512)} %bitcast.424, pred[]{:T(512)} %bitcast.425, pred[]{:T(512)} %bitcast.426, pred[]{:T(512)} %bitcast.427, pred[]{:T(512)} %bitcast.428, pred[]{:T(512)} %bitcast.429, pred[]{:T(512)} %bitcast.430), kind=kLoop, calls=%fused_computation.37.clone.1 | loop fusion | flops 25600 | bytes 1036 | tf_op jit(solution)/shard_map/while/body/eval_jaxpr/and | solution.py:47
  263.1 1.3 pad_maximum_fusion
  267.5 10.3 %fusion.143 = f32[512,8192]{1,0:T(8,128)} fusion(bf16[512,256]{0,1:T(8,128)(2,1)S(1)} %bitcast.441, bf16[256,8192]{1,0:T(8,128)(2,1)} %param.25), kind=kOutput, calls=%fused_computation.229 | convolution fusion | flops 2147483648 | bytes 21233664 | tf_op jit(solution)/shard_map/dot_general | solution.py:229
  277.8 152.3 %reduce-scatter.2.cloned.1.call-done = f32[32,8192]{1,0:T(8,128)} async-done(((f32[512,8192]{1,0:T(8,128)}), f32[32,8192]{1,0:T(8,128)}) %reduce-scatter.2.cloned.1.call-update) | async-done | bytes 1048592 | tf_op jit(solution)/shard_map/reduce_scatter | solution.py:228
  430.2 2.1 convert_element_type.59
  (275 shorter events, 56.8 us)
Async XLA Ops:
  6.5 92.9 %copy-start = (bf16[8192,128]{1,0:T(8,128)(2,1)S(1)}, bf16[8192,128]{1,0:T(8,128)(2,1)}, u32[]{:S(2)}) copy-start(bf16[8192,128]{1,0:T(8,128)(2,1)} %param.24) | copy-start | bytes 6291460
  6.5 10.0 %copy-start.5 = (s32[18,8]{0,1:T(8,128)S(1)}, s32[18,8]{0,1:T(8,128)}, u32[]{:S(2)}) copy-start(s32[18,8]{0,1:T(8,128)} %param.27) | copy-start | bytes 1732
  6.5 9.4 %copy-start.7 = (s32[2]{0:T(128)S(1)}, s32[2]{0:T(128)}, u32[]{:S(2)}) copy-start(s32[2]{0:T(128)} %param.28) | copy-start | bytes 28
  6.5 23.2 %copy-start.10 = (s32[16]{0:T(128)S(1)}, s32[16]{0:T(128)}, u32[]{:S(2)}) copy-start(s32[16]{0:T(128)} %param.29) | copy-start | bytes 196
  6.5 85.7 %all-gather.2.cloned.1.call-start = ((), (), s32[]{:S(2)}) async-start(), calls=%async_computation.1 | async-start | bytes 8912896 | tf_op jit(solution)/shard_map/all_gather | solution.py:170
  10.0 420.1 %reduce-scatter.2.cloned.1.call-start = ((), (), s32[]{:S(2)}) async-start(), calls=%async_computation.2 | async-start | bytes 17825792 | tf_op jit(solution)/shard_map/reduce_scatter | solution.py:228
  15.9 13.9 %copy-start.8 = (f32[64]{0:T(128)}, f32[64]{0:T(128)S(1)}, u32[]{:S(2)}) copy-start(f32[64]{0:T(128)S(1)} %multiply_power_fusion) | copy-start | bytes 772
  99.5 5.7 %copy-start.9 = (f32[64]{0:T(128)S(1)}, f32[64]{0:T(128)}, u32[]{:S(2)}) copy-start(f32[64]{0:T(128)} %copy-done.8) | copy-start | bytes 772
  107.2 3.7 collective-permute-start.2
  110.5 8.9 %collective-permute-start = (bf16[512,2,128]{2,0,1:T(8,128)(2,1)}, bf16[512,2,128]{2,0,1:T(8,128)(2,1)}, u32[]{:S(2)}, u32[]{:S(2)}) collective-permute-start(bf16[512,2,128]{2,0,1:T(8,128)(2,1)} %pad_maximum_fusion.1), channel_id=1, source_target_pairs={{0,1},{1,0},{2,3},{3,2},{4,5},{5,4},{6,7},{7,6},{8,9},{9,8},{10,11... | collective-permute-start | bytes 786440 | tf_op jit(solution)/shard_map/ppermute | solution.py:16
  114.2 6.6 %copy-start.3 = (bf16[1,8,128,256]{3,2,1,0:T(8,128)(2,1)S(1)}, bf16[1,8,128,256]{3,2,1,0:T(8,128)(2,1)}, u32[]{:S(2)}) copy-start(bf16[1,8,128,256]{3,2,1,0:T(8,128)(2,1)} %bitcast_select_fusion.3) | copy-start | bytes 1572868
  121.6 3.0 copy-start.2
  125.4 3.0 copy-start.1
  125.4 3.0 copy-start.11
  128.5 137.9 %copy-start.6 = (f32[512]{0:T(512)S(1)}, f32[512]{0:T(512)}, u32[]{:S(2)}) copy-start(f32[512]{0:T(512)} %pad.16.clone) | copy-start | bytes 6148
  262.5 4.0 copy-start.4
  262.7 2.7 collective-permute-start.1
  264.4 2.1 collective-permute-start.3
  264.8 1.6 collective-permute-start.4
Sparse Core Ops, SparseCore 0:
  10.2 82.0 all-gather.1
  277.9 152.1 reduce-scatter.1
where the time goes:
time: 441 us; the launch traced here: 439 us
  waiting for transfers between devices  212 us (48%)
  other arithmetic  131 us (30%)
  matrix products  41.2 us (9%)
  local copies, waits for them, and re-layouts  38.4 us (9%)
  between operations  13.8 us (3%)
    reduce_scatter x1, waiting for transfers between devices, shards(): lax.psum_scatter(jnp.dot(piece, output_weight, preferred_element_type=jnp...  152 us
    and x18, other arithmetic, cached_block(): jnp.repeat(owned_page, page_len, total_repeat_length=key_span)  99.7 us
    all_gather x1, waiting for transfers between devices, shards(): project_piece = lax.all_gather(normed, 'tensor', axis=0, tiled=True)  58.7 us
    gather x18, local copies, waits for them, and re-layouts, cached_block(): fetched = jnp.take(pool_rows, local_page, axis=1)  12.5 us
    gather x17, local copies, waits for them, and re-layouts, cached_block(): jnp.repeat(owned_page, page_len, total_repeat_length=key_span)  11.4 us
    dot_general x1, matrix products, shards(): jnp.dot(piece, output_weight, preferred_element_type=jnp.float32)  10.3 us
    dynamic_slice x16, local copies, waits for them, and re-layouts, cached_all(): lax.map(decode_one, (queries[2 * stretch_len:], page_table[2:], decode_le...  9.91 us
  transfers between devices with their start and end apart: 7, of which 3 were waited for; matrix products, arithmetic and copies ran while one was open for 8% of the time, Pallas kernels for 0%

commit v1 on v0

--- a/solution.py
+++ b/solution.py
@@ -167,7 +167,9 @@
         * lax.rsqrt(jnp.mean(widened * widened, axis=-1, keepdims=True) + eps_norm)
         * norm_gain
     ).astype(jnp.bfloat16)
-    project_piece = lax.all_gather(normed, "tensor", axis=0, tiled=True)
+    project_piece = jnp.concatenate(
+        lax.all_to_all(jnp.stack([normed] * lax.axis_size("tensor")), "tensor", 0, 0), axis=0
+    )
     joint = jnp.concatenate(
         [
             jnp.dot(project_piece, query_weight, preferred_element_type=jnp.float32),

time: 441 us -> 477 us (1.082)
  waiting for transfers between devices: 212 us -> 243 us
  starting transfers between devices: 1.83 us -> 10.6 us
  local copies, waits for them, and re-layouts: 38.4 us -> 47.1 us
  other arithmetic: 131 us -> 123 us
    all_to_all x0 -> x1, waiting for transfers between devices: none -> 86.3 us  [shards(): lax.all_to_all(jnp.stack([normed] * lax.axis_size('tensor')), 'tensor', 0...]
    all_gather x1 -> x0, waiting for transfers between devices: 58.7 us -> none  [shards(): project_piece = lax.all_gather(normed, 'tensor', axis=0, tiled=True)]
    all_to_all x0 -> x1, starting transfers between devices: none -> 8.45 us  [shards(): lax.all_to_all(jnp.stack([normed] * lax.axis_size('tensor')), 'tensor', 0...]
    dot_general x1, local copies, waits for them, and re-layouts: 0.08 us -> 6.44 us  [shards(): jnp.dot(project_piece, query_weight, preferred_element_type=jnp.float32)]
  transfers between devices with their start and end apart: 7 -> 7, of which waited for: 3 -> 4; matrix products, arithmetic and copies ran while one was open for 8% -> 8% of each run, Pallas kernels for 0% -> 0%
where the time goes in v1:
time: 477 us; the launch traced here: 475 us
  waiting for transfers between devices  243 us (51%)
  other arithmetic  123 us (26%)
  local copies, waits for them, and re-layouts  47.1 us (10%)
  matrix products  36.5 us (8%)
  between operations  13.9 us (3%)
  starting transfers between devices  10.6 us (2%)
    reduce_scatter x1, waiting for transfers between devices, shards(): lax.psum_scatter(jnp.dot(piece, output_weight, preferred_element_type=jnp...  156 us
    and x18, other arithmetic, cached_block(): jnp.repeat(owned_page, page_len, total_repeat_length=key_span)  99.9 us
    all_to_all x1, waiting for transfers between devices, shards(): lax.all_to_all(jnp.stack([normed] * lax.axis_size('tensor')), 'tensor', 0...  86.3 us
    gather x17, local copies, waits for them, and re-layouts, cached_block(): jnp.repeat(owned_page, page_len, total_repeat_length=key_span)  11.8 us
    gather x18, local copies, waits for them, and re-layouts, cached_block(): fetched = jnp.take(pool_rows, local_page, axis=1)  11.2 us
    dynamic_slice x16, local copies, waits for them, and re-layouts, cached_all(): lax.map(decode_one, (queries[2 * stretch_len:], page_table[2:], decode_le...  10.7 us
    dot_general x1, matrix products, shards(): jnp.dot(piece, output_weight, preferred_element_type=jnp.float32)  10.3 us
  transfers between devices with their start and end apart: 7, of which 4 were waited for; matrix products, arithmetic and copies ran while one was open for 8% of the time, Pallas kernels for 0%

profile of v1, /device:TPU:1, one launch (start us, length us, event | category | flops | bytes accessed | tf_op | source)
XLA Modules:
  0.0 475.1 jit_solution(9375246451662992713)
XLA Ops:
  6.5 1.4 fusion.62
  7.9 1.2 fusion.64
  9.2 4.2 stack.2
  13.4 8.4 %all-to-all-start = ((bf16[16,32,8192]{2,1,0:T(8,128)(2,1)}), bf16[16,32,8192]{2,1,0:T(8,128)(2,1)}, u32[]{:S(2)}, u32[]{:S(2)}) async-start(bf16[16,32,8192]{2,1,0:T(8,128)(2,1)} %stack.2), calls=%async_computation | async-start | bytes 16777216 | tf_op jit(solution)/shard_map/all_to_all | solution.py:171
  22.0 6.4 %copy.47 = bf16[256,8192]{1,0:T(8,128)(2,1)} copy(bf16[256,8192]{0,1:T(8,128)(2,1)} %bitcast.438) | data formatting | bytes 8388608 | tf_op jit(solution)/shard_map/dot_general | solution.py:175
  29.4 1.4 gather_fusion.1
  32.3 0.7 fusion.132
  33.0 5.4 %fusion.115 = pred[1024]{0:T(1024)(128)(4,1)S(1)} fusion(s32[]{:T(128)} %bitcast.46, pred[]{:T(512)} %bitcast.58, pred[]{:T(512)} %bitcast.57, pred[]{:T(512)} %bitcast.56, pred[]{:T(512)} %bitcast.55, pred[]{:T(512)} %bitcast.54, pred[]{:T(512)} %bitcast.53, pred[]{:T(512)} %bitcast.52, pred[]{:T(512)} %bitcast.51), kind=kLoop, calls=%fused_computation.187 | loop fusion | flops 25600 | bytes 1036 | tf_op jit(solution)/shard_map/and | solution.py:47
  38.3 5.8 %fusion.114 = pred[1024]{0:T(1024)(128)(4,1)S(1)} fusion(s32[]{:T(128)} %bitcast.36, pred[]{:T(512)} %bitcast.35, pred[]{:T(512)} %bitcast.34, pred[]{:T(512)} %bitcast.33, pred[]{:T(512)} %bitcast.32, pred[]{:T(512)} %bitcast.31, pred[]{:T(512)} %bitcast.30, pred[]{:T(512)} %bitcast.29, pred[]{:T(512)} %bitcast.28), kind=kLoop, calls=%fused_computation.186 | loop fusion | flops 25600 | bytes 1036 | tf_op jit(solution)/shard_map/and | solution.py:47
  44.1 1.3 iota_add_fusion
  46.1 0.9 bitcast_select_fusion.3
  47.0 1.2 bitcast_select_fusion.4
  48.1 86.3 %all-to-all-done = bf16[16,32,8192]{2,1,0:T(8,128)(2,1)} async-done(((bf16[16,32,8192]{2,1,0:T(8,128)(2,1)}), bf16[16,32,8192]{2,1,0:T(8,128)(2,1)}, u32[]{:S(2)}, u32[]{:S(2)}) %all-to-all-start) | async-done | bytes 8388640 | tf_op jit(solution)/shard_map/all_to_all | solution.py:171
  134.5 5.9 %fusion.138 = f32[512,128]{1,0:T(8,128)S(1)} fusion(bf16[512,8192]{1,0:T(8,128)(2,1)} %bitcast.42, bf16[8192,128]{1,0:T(8,128)(2,1)S(1)} %copy-done), kind=kOutput, calls=%fused_computation.225 | convolution fusion | flops 1073741824 | bytes 10747904 | tf_op jit(solution)/shard_map/dot_general | solution.py:176
  140.3 1.2 fusion.76
  142.4 5.7 %fusion.137 = f32[512,2,128]{0,2,1:T(8,128)S(1)} fusion(bf16[512,8192,1]{1,0,2:T(8,128)(2,1)} %bitcast.43, bf16[2,128,8192]{2,1,0:T(8,128)(2,1)S(1)} %bitcast.439), kind=kOutput, calls=%fused_computation.224 | convolution fusion | flops 2147483648 | bytes 13107200 | tf_op jit(solution)/shard_map/dot_general | solution.py:175
  148.2 0.7 pad_maximum_fusion.1
  150.3 1.1 convolution_bitcast_fusion.1
  152.1 1.1 maximum_select_fusion
  153.4 0.9 bitcast_reduce_fusion
  154.3 1.8 fusion.54
  156.2 1.2 fusion.40
  157.3 0.9 bitcast_reduce_fusion.1
  158.2 1.1 fusion.57
  159.3 1.2 fusion.38
  160.6 135.1 %while.21 = (s32[]{:T(128)}, f32[16,1,1,4]{3,2,1,0:T(1,128)S(1)}, f32[16,1,1,4]{3,2,1,0:T(1,128)S(1)}, f32[16,1,1,4,128]{4,0,3,2,1:T(8,128)S(1)}, s32[16,8]{1,0:...) while((s32[]{:T(128)}, f32[16,1,1,4]{3,2,1,0:T(1,128)S(1)}, ...), condition=%wide.region_6.9_spmd, body=%wide.region_3.8_spmd.sunk | while | flops 2422874 | bytes 2688929 | solution.py:86
  162.7 5.5 %fusion.154 = pred[1024]{0:T(1024)(128)(4,1)S(1)} fusion(s32[]{:T(128)} %bitcast.424, pred[]{:T(512)} %bitcast.425, pred[]{:T(512)} %bitcast.426, pred[]{:T(512)} %bitcast.427, pred[]{:T(512)} %bitcast.428, pred[]{:T(512)} %bitcast.429, pred[]{:T(512)} %bitcast.430, pred[]{:T(512)} %bitcast.431, pred[]{:T(512)} %bitcast.432), kind=kLoop, calls=%fused_computation.37.clone.1 | loop fusion | flops 25600 | bytes 1036 | tf_op jit(solution)/shard_map/while/body/eval_jaxpr/and | solution.py:47
  170.4 0.7 fusion.153
  171.1 5.5 %fusion.154 = pred[1024]{0:T(1024)(128)(4,1)S(1)} fusion(s32[]{:T(128)} %bitcast.424, pred[]{:T(512)} %bitcast.425, pred[]{:T(512)} %bitcast.426, pred[]{:T(512)} %bitcast.427, pred[]{:T(512)} %bitcast.428, pred[]{:T(512)} %bitcast.429, pred[]{:T(512)} %bitcast.430, pred[]{:T(512)} %bitcast.431, pred[]{:T(512)} %bitcast.432), kind=kLoop, calls=%fused_computation.37.clone.1 | loop fusion | flops 25600 | bytes 1036 | tf_op jit(solution)/shard_map/while/body/eval_jaxpr/and | solution.py:47
  179.6 5.5 %fusion.154 = pred[1024]{0:T(1024)(128)(4,1)S(1)} fusion(s32[]{:T(128)} %bitcast.424, pred[]{:T(512)} %bitcast.425, pred[]{:T(512)} %bitcast.426, pred[]{:T(512)} %bitcast.427, pred[]{:T(512)} %bitcast.428, pred[]{:T(512)} %bitcast.429, pred[]{:T(512)} %bitcast.430, pred[]{:T(512)} %bitcast.431, pred[]{:T(512)} %bitcast.432), kind=kLoop, calls=%fused_computation.37.clone.1 | loop fusion | flops 25600 | bytes 1036 | tf_op jit(solution)/shard_map/while/body/eval_jaxpr/and | solution.py:47
  188.0 5.5 %fusion.154 = pred[1024]{0:T(1024)(128)(4,1)S(1)} fusion(s32[]{:T(128)} %bitcast.424, pred[]{:T(512)} %bitcast.425, pred[]{:T(512)} %bitcast.426, pred[]{:T(512)} %bitcast.427, pred[]{:T(512)} %bitcast.428, pred[]{:T(512)} %bitcast.429, pred[]{:T(512)} %bitcast.430, pred[]{:T(512)} %bitcast.431, pred[]{:T(512)} %bitcast.432), kind=kLoop, calls=%fused_computation.37.clone.1 | loop fusion | flops 25600 | bytes 1036 | tf_op jit(solution)/shard_map/while/body/eval_jaxpr/and | solution.py:47
  196.5 5.5 %fusion.154 = pred[1024]{0:T(1024)(128)(4,1)S(1)} fusion(s32[]{:T(128)} %bitcast.424, pred[]{:T(512)} %bitcast.425, pred[]{:T(512)} %bitcast.426, pred[]{:T(512)} %bitcast.427, pred[]{:T(512)} %bitcast.428, pred[]{:T(512)} %bitcast.429, pred[]{:T(512)} %bitcast.430, pred[]{:T(512)} %bitcast.431, pred[]{:T(512)} %bitcast.432), kind=kLoop, calls=%fused_computation.37.clone.1 | loop fusion | flops 25600 | bytes 1036 | tf_op jit(solution)/shard_map/while/body/eval_jaxpr/and | solution.py:47
  204.9 5.5 %fusion.154 = pred[1024]{0:T(1024)(128)(4,1)S(1)} fusion(s32[]{:T(128)} %bitcast.424, pred[]{:T(512)} %bitcast.425, pred[]{:T(512)} %bitcast.426, pred[]{:T(512)} %bitcast.427, pred[]{:T(512)} %bitcast.428, pred[]{:T(512)} %bitcast.429, pred[]{:T(512)} %bitcast.430, pred[]{:T(512)} %bitcast.431, pred[]{:T(512)} %bitcast.432), kind=kLoop, calls=%fused_computation.37.clone.1 | loop fusion | flops 25600 | bytes 1036 | tf_op jit(solution)/shard_map/while/body/eval_jaxpr/and | solution.py:47
  213.4 5.5 %fusion.154 = pred[1024]{0:T(1024)(128)(4,1)S(1)} fusion(s32[]{:T(128)} %bitcast.424, pred[]{:T(512)} %bitcast.425, pred[]{:T(512)} %bitcast.426, pred[]{:T(512)} %bitcast.427, pred[]{:T(512)} %bitcast.428, pred[]{:T(512)} %bitcast.429, pred[]{:T(512)} %bitcast.430, pred[]{:T(512)} %bitcast.431, pred[]{:T(512)} %bitcast.432), kind=kLoop, calls=%fused_computation.37.clone.1 | loop fusion | flops 25600 | bytes 1036 | tf_op jit(solution)/shard_map/while/body/eval_jaxpr/and | solution.py:47
  221.8 5.5 %fusion.154 = pred[1024]{0:T(1024)(128)(4,1)S(1)} fusion(s32[]{:T(128)} %bitcast.424, pred[]{:T(512)} %bitcast.425, pred[]{:T(512)} %bitcast.426, pred[]{:T(512)} %bitcast.427, pred[]{:T(512)} %bitcast.428, pred[]{:T(512)} %bitcast.429, pred[]{:T(512)} %bitcast.430, pred[]{:T(512)} %bitcast.431, pred[]{:T(512)} %bitcast.432), kind=kLoop, calls=%fused_computation.37.clone.1 | loop fusion | flops 25600 | bytes 1036 | tf_op jit(solution)/shard_map/while/body/eval_jaxpr/and | solution.py:47
  230.3 5.5 %fusion.154 = pred[1024]{0:T(1024)(128)(4,1)S(1)} fusion(s32[]{:T(128)} %bitcast.424, pred[]{:T(512)} %bitcast.425, pred[]{:T(512)} %bitcast.426, pred[]{:T(512)} %bitcast.427, pred[]{:T(512)} %bitcast.428, pred[]{:T(512)} %bitcast.429, pred[]{:T(512)} %bitcast.430, pred[]{:T(512)} %bitcast.431, pred[]{:T(512)} %bitcast.432), kind=kLoop, calls=%fused_computation.37.clone.1 | loop fusion | flops 25600 | bytes 1036 | tf_op jit(solution)/shard_map/while/body/eval_jaxpr/and | solution.py:47
  238.7 5.5 %fusion.154 = pred[1024]{0:T(1024)(128)(4,1)S(1)} fusion(s32[]{:T(128)} %bitcast.424, pred[]{:T(512)} %bitcast.425, pred[]{:T(512)} %bitcast.426, pred[]{:T(512)} %bitcast.427, pred[]{:T(512)} %bitcast.428, pred[]{:T(512)} %bitcast.429, pred[]{:T(512)} %bitcast.430, pred[]{:T(512)} %bitcast.431, pred[]{:T(512)} %bitcast.432), kind=kLoop, calls=%fused_computation.37.clone.1 | loop fusion | flops 25600 | bytes 1036 | tf_op jit(solution)/shard_map/while/body/eval_jaxpr/and | solution.py:47
  247.1 5.5 %fusion.154 = pred[1024]{0:T(1024)(128)(4,1)S(1)} fusion(s32[]{:T(128)} %bitcast.424, pred[]{:T(512)} %bitcast.425, pred[]{:T(512)} %bitcast.426, pred[]{:T(512)} %bitcast.427, pred[]{:T(512)} %bitcast.428, pred[]{:T(512)} %bitcast.429, pred[]{:T(512)} %bitcast.430, pred[]{:T(512)} %bitcast.431, pred[]{:T(512)} %bitcast.432), kind=kLoop, calls=%fused_computation.37.clone.1 | loop fusion | flops 25600 | bytes 1036 | tf_op jit(solution)/shard_map/while/body/eval_jaxpr/and | solution.py:47
  255.6 5.5 %fusion.154 = pred[1024]{0:T(1024)(128)(4,1)S(1)} fusion(s32[]{:T(128)} %bitcast.424, pred[]{:T(512)} %bitcast.425, pred[]{:T(512)} %bitcast.426, pred[]{:T(512)} %bitcast.427, pred[]{:T(512)} %bitcast.428, pred[]{:T(512)} %bitcast.429, pred[]{:T(512)} %bitcast.430, pred[]{:T(512)} %bitcast.431, pred[]{:T(512)} %bitcast.432), kind=kLoop, calls=%fused_computation.37.clone.1 | loop fusion | flops 25600 | bytes 1036 | tf_op jit(solution)/shard_map/while/body/eval_jaxpr/and | solution.py:47
  264.0 5.5 %fusion.154 = pred[1024]{0:T(1024)(128)(4,1)S(1)} fusion(s32[]{:T(128)} %bitcast.424, pred[]{:T(512)} %bitcast.425, pred[]{:T(512)} %bitcast.426, pred[]{:T(512)} %bitcast.427, pred[]{:T(512)} %bitcast.428, pred[]{:T(512)} %bitcast.429, pred[]{:T(512)} %bitcast.430, pred[]{:T(512)} %bitcast.431, pred[]{:T(512)} %bitcast.432), kind=kLoop, calls=%fused_computation.37.clone.1 | loop fusion | flops 25600 | bytes 1036 | tf_op jit(solution)/shard_map/while/body/eval_jaxpr/and | solution.py:47
  272.5 5.5 %fusion.154 = pred[1024]{0:T(1024)(128)(4,1)S(1)} fusion(s32[]{:T(128)} %bitcast.424, pred[]{:T(512)} %bitcast.425, pred[]{:T(512)} %bitcast.426, pred[]{:T(512)} %bitcast.427, pred[]{:T(512)} %bitcast.428, pred[]{:T(512)} %bitcast.429, pred[]{:T(512)} %bitcast.430, pred[]{:T(512)} %bitcast.431, pred[]{:T(512)} %bitcast.432), kind=kLoop, calls=%fused_computation.37.clone.1 | loop fusion | flops 25600 | bytes 1036 | tf_op jit(solution)/shard_map/while/body/eval_jaxpr/and | solution.py:47
  280.9 5.5 %fusion.154 = pred[1024]{0:T(1024)(128)(4,1)S(1)} fusion(s32[]{:T(128)} %bitcast.424, pred[]{:T(512)} %bitcast.425, pred[]{:T(512)} %bitcast.426, pred[]{:T(512)} %bitcast.427, pred[]{:T(512)} %bitcast.428, pred[]{:T(512)} %bitcast.429, pred[]{:T(512)} %bitcast.430, pred[]{:T(512)} %bitcast.431, pred[]{:T(512)} %bitcast.432), kind=kLoop, calls=%fused_computation.37.clone.1 | loop fusion | flops 25600 | bytes 1036 | tf_op jit(solution)/shard_map/while/body/eval_jaxpr/and | solution.py:47
  289.4 5.5 %fusion.154 = pred[1024]{0:T(1024)(128)(4,1)S(1)} fusion(s32[]{:T(128)} %bitcast.424, pred[]{:T(512)} %bitcast.425, pred[]{:T(512)} %bitcast.426, pred[]{:T(512)} %bitcast.427, pred[]{:T(512)} %bitcast.428, pred[]{:T(512)} %bitcast.429, pred[]{:T(512)} %bitcast.430, pred[]{:T(512)} %bitcast.431, pred[]{:T(512)} %bitcast.432), kind=kLoop, calls=%fused_computation.37.clone.1 | loop fusion | flops 25600 | bytes 1036 | tf_op jit(solution)/shard_map/while/body/eval_jaxpr/and | solution.py:47
  296.8 0.8 collective-permute-start.4
  298.6 0.9 fusion.67
  299.6 10.3 %fusion.139 = f32[512,8192]{1,0:T(8,128)} fusion(bf16[512,256]{0,1:T(8,128)(2,1)S(1)} %bitcast.445, bf16[256,8192]{1,0:T(8,128)(2,1)} %param.25), kind=kOutput, calls=%fused_computation.226 | convolution fusion | flops 2147483648 | bytes 21233664 | tf_op jit(solution)/shard_map/dot_general | solution.py:231
  309.9 156.3 %reduce-scatter.2.cloned.1.call-done = f32[32,8192]{1,0:T(8,128)} async-done(((f32[512,8192]{1,0:T(8,128)}), f32[32,8192]{1,0:T(8,128)}) %reduce-scatter.2.cloned.1.call-update) | async-done | bytes 1048592 | tf_op jit(solution)/shard_map/reduce_scatter | solution.py:230
  466.2 2.1 convert_element_type.59
  (276 shorter events, 53.0 us)
Async XLA Ops:
  6.5 127.9 %copy-start = (bf16[8192,128]{1,0:T(8,128)(2,1)S(1)}, bf16[8192,128]{1,0:T(8,128)(2,1)}, u32[]{:S(2)}) copy-start(bf16[8192,128]{1,0:T(8,128)(2,1)} %param.24) | copy-start | bytes 6291460
  13.4 121.0 %all-to-all-start = ((bf16[16,32,8192]{2,1,0:T(8,128)(2,1)}), bf16[16,32,8192]{2,1,0:T(8,128)(2,1)}, u32[]{:S(2)}, u32[]{:S(2)}) async-start(bf16[16,32,8192]{2,1,0:T(8,128)(2,1)} %stack.2), calls=%async_computation | async-start | bytes 16777216 | tf_op jit(solution)/shard_map/all_to_all | solution.py:171
  21.9 444.3 %reduce-scatter.2.cloned.1.call-start = ((), (), s32[]{:S(2)}) async-start(), calls=%async_computation.2 | async-start | bytes 17825792 | tf_op jit(solution)/shard_map/reduce_scatter | solution.py:230
  22.0 6.5 %copy-start.7 = (s32[18,8]{0,1:T(8,128)S(1)}, s32[18,8]{0,1:T(8,128)}, u32[]{:S(2)}) copy-start(s32[18,8]{0,1:T(8,128)} %param.27) | copy-start | bytes 1732
  22.0 6.8 %copy-start.2 = (bf16[8,128,256]{2,1,0:T(8,128)(2,1)S(1)}, bf16[8,128,256]{2,1,0:T(8,128)(2,1)}, u32[]{:S(2)}) copy-start(bf16[8,128,256]{2,1,0:T(8,128)(2,1)} %param.26) | copy-start | bytes 1572868
  22.0 9.5 %copy-start.9 = (s32[2]{0:T(128)S(1)}, s32[2]{0:T(128)}, u32[]{:S(2)}) copy-start(s32[2]{0:T(128)} %param.28) | copy-start | bytes 28
  22.0 23.4 %copy-start.12 = (s32[16]{0:T(128)S(1)}, s32[16]{0:T(128)}, u32[]{:S(2)}) copy-start(s32[16]{0:T(128)} %param.29) | copy-start | bytes 196
  31.5 14.0 %copy-start.10 = (f32[64]{0:T(128)}, f32[64]{0:T(128)S(1)}, u32[]{:S(2)}) copy-start(f32[64]{0:T(128)S(1)} %multiply_power_fusion) | copy-start | bytes 772
  134.5 5.9 %copy-start.11 = (f32[64]{0:T(128)S(1)}, f32[64]{0:T(128)}, u32[]{:S(2)}) copy-start(f32[64]{0:T(128)} %copy-done.10) | copy-start | bytes 772
  134.5 7.9 %copy-start.3 = (bf16[256,8192]{1,0:T(8,128)(2,1)S(1)}, bf16[256,8192]{1,0:T(8,128)(2,1)}, u32[]{:S(2)}) copy-start(bf16[256,8192]{1,0:T(8,128)(2,1)} %copy.47) | copy-start | bytes 12582916
  141.7 7.3 %collective-permute-start.2 = (bf16[512,128]{1,0:T(8,128)(2,1)S(1)}, bf16[512,128]{1,0:T(8,128)(2,1)S(1)}, u32[]{:S(2)}, u32[]{:S(2)}) collective-permute-start(bf16[512,128]{1,0:T(8,128)(2,1)S(1)} %fusion.83), channel_id=1, source_target_pairs={{0,1},{1,0},{2,3},{3,2},{4,5},{5,4},{6,7},{7,6},{8,9},{9,8},{10,11... | collective-permute-start | bytes 393224 | tf_op jit(solution)/shard_map/ppermute | solution.py:16
  148.2 5.2 %copy-start.4 = (bf16[1,8,128,256]{3,2,1,0:T(8,128)(2,1)S(1)}, bf16[1,8,128,256]{3,2,1,0:T(8,128)(2,1)}, u32[]{:S(2)}) copy-start(bf16[1,8,128,256]{3,2,1,0:T(8,128)(2,1)} %bitcast_select_fusion.3) | copy-start | bytes 1572868
  148.9 3.2 collective-permute-start
  149.0 1.1 copy-start.5
  159.3 1.3 copy-start.13
  160.5 135.1 %copy-start.6 = (f32[248,1,4,128]{3,0,2,1:T(8,128)S(1)}, f32[248,1,4,128]{3,0,2,1:T(8,128)}, u32[]{:S(2)}) copy-start(f32[248,1,4,128]{3,0,2,1:T(8,128)} %fusion.54) | copy-start | bytes 1523716
  160.6 137.9 %copy-start.8 = (f32[512]{0:T(512)S(1)}, f32[512]{0:T(512)}, u32[]{:S(2)}) copy-start(f32[512]{0:T(512)} %pad.16.clone) | copy-start | bytes 6148
  295.8 2.7 collective-permute-start.3
  296.6 1.4 collective-permute-start.1
  296.8 1.6 collective-permute-start.4
  309.9 158.4 %copy-start.1 = (bf16[8192,128]{1,0:T(8,128)(2,1)S(1)}, bf16[8192,128]{1,0:T(8,128)(2,1)}, u32[]{:S(2)}) copy-start(bf16[8192,128]{1,0:T(8,128)(2,1)} %param.24) | copy-start | bytes 6291460
Sparse Core Ops, SparseCore 0:
  310.0 156.1 reduce-scatter.1
